TPU v7x, 256 devices: a whole 4x4x8 slice. The times are simulated.
256 devices in a mesh: ctx: 32 (over z, y_hi, core), fsdp: 8 (over x, y_lo).
Axes of the slice: x: 4, y: 4 (y_hi: 2, y_lo: 2; y = y_hi * 2 + y_lo), z: 8, core: 2. Of those that a mesh axis runs over, the one named last changes fastest.
Arguments:
- xbc_raw: bfloat16 [8, 4096, 2560], P('fsdp', 'ctx'), may hold values from -6 to 6
- dt_raw: float32 [8, 4096, 64], P('fsdp', 'ctx'), as said below
- a_log: float32 [64], replicated, may hold values from 0 to 2.7726, as said below
- skip: float32 [64], replicated, may hold values from 0.5 to 1.5
- conv_weight: bfloat16 [4, 2560], P(None, 'fsdp'), may hold values from -3 to 3
- conv_bias: bfloat16 [2560], P('fsdp'), may hold values from -3 to 3
- grad_y: bfloat16 [8, 4096, 2048], P('fsdp', 'ctx'), may hold values from -6 to 6
Outputs:
- grad_xbc_raw: bfloat16 [8, 4096, 2560], P('fsdp', 'ctx')
- grad_dt_raw: float32 [8, 4096, 64], P('fsdp', 'ctx')
- grad_a_log: float32 [64], replicated
- grad_skip: float32 [64], replicated
- grad_conv_weight: float32 [4, 2560], P(None, 'fsdp')
- grad_conv_bias: float32 [2560], P('fsdp')
Inputs may be any that keep to these rules, and one draw needn't show every extreme that they name: Each head's decay coefficient exp(a_log) lies between 1 and 16. softplus(dt_raw) is a positive step size.
All inputs are finite; a program needn't handle non-finite values.
Results may differ from a plain program's by a relative error of at most 0.0007.
Values may be sent and summed in bfloat16 or wider, within the bound.
A program may use at most 256 MiB of HBM per device.

v0:
```python
import math
import jax
import jax.numpy as jnp
from jax import lax
from jax.sharding import PartitionSpec as P

HW = 64
GW = 4
P_SIZE = 32
N = 64
KW = 4
SPAN = 128
HIGHEST_PREC = lax.Precision.HIGHEST


def from_behind(value, axis, by):
    length = lax.axis_size(axis)
    pairs = [(i, i + by) for i in range(length) if 0 <= i + by < length]
    return lax.ppermute(value, axis, pairs)


def compose(earlier, later):
    return (earlier[0] * later[0], later[0][..., None, None] * earlier[1] + later[1])


def exclusive_scans(fwd, bwd, axis):
    count = lax.axis_size(axis)
    width = 1
    while 2 * width < count:
        fwd = compose(from_behind(fwd, axis, width), fwd)
        bwd = compose(from_behind(bwd, axis, -width), bwd)
        width *= 2
    fwd_near = from_behind(fwd, axis, 1)
    bwd_near = from_behind(bwd, axis, -1)
    if width + 1 < count:
        fwd = compose(from_behind(fwd, axis, width + 1), fwd_near)
        bwd = compose(from_behind(bwd, axis, -(width + 1)), bwd_near)
    else:
        fwd, bwd = (fwd_near, bwd_near)
    return (fwd[1], bwd[1])


def body(xbc_raw, dt_raw, a_log, skip, conv_weight, conv_bias, grad_y):
    raw_rows = xbc_raw[0]
    tok_rows = raw_rows.shape[0]
    per_group = HW // GW
    inner_width = HW * P_SIZE
    blocks = tok_rows // SPAN
    params_all = lax.all_gather(
        jnp.concatenate([conv_weight, conv_bias[None]], 0), "fsdp", axis=1, tiled=True
    ).astype(jnp.float32)
    weight_f = params_all[:KW]
    bias_f = params_all[KW]
    tail_rows = raw_rows[tok_rows - (KW - 1) :]
    rows_prev = from_behind(tail_rows, "ctx", 1)
    padded = jnp.concatenate([rows_prev, raw_rows], 0).astype(jnp.float32)
    pre_act = bias_f + sum(
        (weight_f[tap_idx] * padded[tap_idx : tap_idx + tok_rows] for tap_idx in range(KW))
    )
    gate_vals = jax.nn.sigmoid(pre_act)
    conv_out = pre_act * gate_vals
    x_all = conv_out[:, :inner_width].reshape(blocks, SPAN, GW, per_group, P_SIZE)
    b_all = conv_out[:, inner_width : inner_width + GW * N].reshape(blocks, SPAN, GW, N)
    c_all = conv_out[:, inner_width + GW * N :].reshape(blocks, SPAN, GW, N)
    steps_raw = dt_raw[0]
    step_size = jax.nn.softplus(steps_raw)
    rate_head = jnp.exp(a_log)
    log_decay = -rate_head * step_size
    dt_c = step_size.reshape(blocks, SPAN, GW, per_group)
    la_c = log_decay.reshape(blocks, SPAN, GW, per_group)
    d_out = grad_y[0].astype(jnp.float32).reshape(blocks, SPAN, GW, per_group, P_SIZE)
    cum_log = jnp.cumsum(la_c, 1)
    exp_cum = jnp.exp(cum_log)
    last_log = cum_log[:, -1]
    span_decay = jnp.exp(last_log)
    tail_decay = jnp.exp(last_log[:, None] - cum_log)
    inputs = dt_c[..., None] * x_all
    local_end = jnp.einsum(
        "csgkp,csgn->cgkpn", tail_decay[..., None] * inputs, b_all, precision=HIGHEST_PREC
    )
    local_adj = jnp.einsum(
        "ctgkp,ctgn->cgkpn", exp_cum[..., None] * d_out, c_all, precision=HIGHEST_PREC
    )
    unit_decay = jnp.ones((GW, per_group), jnp.float32)
    zero_state = jnp.zeros((GW, per_group, P_SIZE, N), jnp.float32)
    dev_decay = unit_decay
    fwd_total = zero_state
    span_idx = 0
    fwd_total = span_decay[span_idx][..., None, None] * fwd_total + local_end[span_idx]
    dev_decay = dev_decay * span_decay[span_idx]
    back_total = zero_state
    for span_idx in reversed(range(blocks)):
        back_total = local_adj[span_idx] + span_decay[span_idx][..., None, None] * back_total
    state_in, adjoint_end = exclusive_scans((dev_decay, fwd_total), (dev_decay, back_total), "ctx")
    cum_t = jnp.transpose(cum_log, (0, 2, 3, 1))
    lower_mask = jnp.tril(jnp.ones((SPAN, SPAN), bool))
    log_gap = cum_t[..., :, None] - cum_t[..., None, :]
    mixing = jnp.where(lower_mask, jnp.exp(jnp.where(lower_mask, log_gap, 0.0)), 0.0)
    scores = jnp.einsum("ctgn,csgn->cgts", c_all, b_all, precision=HIGHEST_PREC)
    weights = scores[:, :, None] * mixing
    d_weights = jnp.einsum("ctgkp,csgkp->cgkts", d_out, inputs, precision=HIGHEST_PREC)
    d_inputs = jnp.einsum("cgkts,ctgkp->csgkp", weights, d_out, precision=HIGHEST_PREC)
    flow_terms = d_weights * weights
    d_scores = jnp.sum(d_weights * mixing, 2)
    d_cum = jnp.transpose(jnp.sum(flow_terms, -1) - jnp.sum(flow_terms, -2), (0, 3, 1, 2))
    d_c = jnp.einsum("cgts,csgn->ctgn", d_scores, b_all, precision=HIGHEST_PREC)
    d_b = jnp.einsum("cgts,ctgn->csgn", d_scores, c_all, precision=HIGHEST_PREC)
    carried = state_in
    span_idx = 0
    start_list = [carried]
    end_list = []
    carried = adjoint_end
    for span_idx in reversed(range(blocks)):
        end_list.append(carried)
        carried = local_adj[span_idx] + span_decay[span_idx][..., None, None] * carried
    start_state = jnp.stack(start_list)
    end_adjoint = jnp.stack(end_list[::-1])
    from_state = jnp.einsum("ctgn,cgkpn->ctgkp", c_all, start_state, precision=HIGHEST_PREC)
    d_cum = d_cum + exp_cum * jnp.sum(d_out * from_state, -1)
    d_c = d_c + jnp.einsum(
        "ctgkp,cgkpn->ctgn", exp_cum[..., None] * d_out, start_state, precision=HIGHEST_PREC
    )
    pulled = jnp.einsum("cgkpn,csgn->csgkp", end_adjoint, b_all, precision=HIGHEST_PREC)
    d_inputs = d_inputs + tail_decay[..., None] * pulled
    d_b = d_b + jnp.einsum(
        "csgkp,cgkpn->csgn", tail_decay[..., None] * inputs, end_adjoint, precision=HIGHEST_PREC
    )
    d_tail = tail_decay * jnp.sum(inputs * pulled, -1)
    d_last = jnp.sum(d_tail, 1) + span_decay * jnp.sum(end_adjoint * start_state, (-2, -1))
    d_cum = d_cum - d_tail
    d_cum = d_cum.at[:, -1].add(d_last)
    d_log = jnp.flip(jnp.cumsum(jnp.flip(d_cum, 1), 1), 1)
    d_step = jnp.sum(d_inputs * x_all, -1) - rate_head.reshape(GW, per_group) * d_log
    d_x = d_inputs * dt_c[..., None] + skip.reshape(GW, per_group)[..., None] * d_out
    d_skip_local = jnp.sum(d_out * x_all, (0, 1, 4)).reshape(HW)
    d_alog_local = jnp.sum(d_log * la_c, (0, 1)).reshape(HW)
    d_dt_raw = d_step.reshape(tok_rows, HW) * jax.nn.sigmoid(steps_raw)
    d_conv = jnp.concatenate(
        [
            d_x.reshape(tok_rows, inner_width),
            d_b.reshape(tok_rows, GW * N),
            d_c.reshape(tok_rows, GW * N),
        ],
        1,
    )
    d_pre = d_conv * gate_vals * (1.0 + pre_act * (1.0 - gate_vals))
    rows_next = from_behind(d_pre[: KW - 1], "ctx", -1)
    extended = jnp.concatenate([d_pre, rows_next], 0)
    d_raw = sum(
        (
            weight_f[tap_idx] * extended[KW - 1 - tap_idx : KW - 1 - tap_idx + tok_rows]
            for tap_idx in range(KW)
        )
    )
    d_weight = jnp.stack(
        [jnp.sum(d_pre * padded[tap_idx : tap_idx + tok_rows], 0) for tap_idx in range(KW)]
    )
    d_bias = jnp.sum(d_pre, 0)
    grad_scale = 1.0 / math.sqrt(tok_rows * lax.axis_size("ctx") * lax.axis_size("fsdp"))
    channels = d_bias.shape[0]
    packed = jnp.concatenate([d_weight.reshape(-1), d_bias, d_alog_local, d_skip_local])
    packed = lax.psum(packed, ("ctx", "fsdp"))
    own = channels // lax.axis_size("fsdp")
    col0 = lax.axis_index("fsdp") * own
    wb = packed[: (KW + 1) * channels].reshape(KW + 1, channels)
    wb_own = lax.dynamic_slice_in_dim(wb, col0, own, axis=1)
    total_weight, total_bias = (wb_own[:KW], wb_own[KW])
    heads_part = packed[(KW + 1) * channels :]
    head_alog, head_skip = (heads_part[:HW], heads_part[HW:])
    return (
        d_raw.astype(jnp.bfloat16)[None],
        d_dt_raw[None],
        head_alog * grad_scale,
        head_skip * grad_scale,
        total_weight * grad_scale,
        total_bias * grad_scale,
    )


def solution(mesh):
    in_specs = (
        P("fsdp", "ctx", None),
        P("fsdp", "ctx", None),
        P(),
        P(),
        P(None, "fsdp"),
        P("fsdp"),
        P("fsdp", "ctx", None),
    )
    out_specs = (
        P("fsdp", "ctx", None),
        P("fsdp", "ctx", None),
        P(),
        P(),
        P(None, "fsdp"),
        P("fsdp"),
    )
    return jax.shard_map(body, mesh=mesh, in_specs=in_specs, out_specs=out_specs, check_vma=False)
```

profile of v0, /device:TPU:1, one launch (start us, length us, event | category | flops | bytes accessed | tf_op | source)
XLA Modules:
  0.0 447.0 jit_solution(13302643420018480362)
XLA Ops:
  3.4 5.1 %collective-permute-start.1 = (f32[4,16]{1,0:T(4,128)S(1)}, f32[4,16]{1,0:T(4,128)S(1)}, u32[]{:S(2)}, u32[]{:S(2)}) collective-permute-start(f32[4,16]{1,0:T(4,128)S(1)} %exp.91), channel_id=1, source_target_pairs={{8,0},{16,8},{24,16},{32,24},{40,32},{48,40},{56,48},{64,56},{72,6... | collective-permute-start | bytes 776 | tf_op jit(solution)/shard_map/ppermute | solution.py:19
  8.5 3.0 collective-permute-start.12
  12.4 2.4 collective-permute-start
  15.4 22.3 %all-gather = bf16[8,320,5]{1,2,0:T(8,128)(2,1)S(1)} all-gather(bf16[1,320,5]{1,2,0:T(8,128)(2,1)S(1)} %maximum_bitcast_fusion), channel_id=1, replica_groups=mesh['ctx'=32,'fsdp'=8] {'fsdp'}, dimensions={0}, use_global_device_ids=true | all-gather | bytes 28800 | tf_op jit(solution)/shard_map/all_gather | solution.py:49
  43.1 4.0 fusion.25
  49.1 11.6 %collective-permute-start.17 = (f32[4,16,32,64]{3,2,1,0:T(8,128)S(1)}, f32[4,16,32,64]{3,2,1,0:T(8,128)S(1)}, u32[]{:S(2)}, u32[]{:S(2)}) collective-permute-start(f32[4,16,32,64]{3,2,1,0:T(8,128)S(1)} %convolution_add_fusion), channel_id=1, source_target_pairs={{0,8},{8,16},{16,24},{24,32},{32,40},{40,48},{48,56},{56,64},{64,7... | collective-permute-start | bytes 1572872 | tf_op jit(solution)/shard_map/ppermute | solution.py:19
  63.7 19.9 %collective-permute-done.17 = f32[4,16,32,64]{3,2,1,0:T(8,128)S(1)} collective-permute-done((f32[4,16,32,64]{3,2,1,0:T(8,128)S(1)}, f32[4,16,32,64]{3,2,1,0:T(8,128)S(1)}, u32[]{:S(2)}, u32[]{:S(2)}) %collective-permute-start.17) | collective-permute-done | bytes 524320 | tf_op jit(solution)/shard_map/ppermute | solution.py:19
  85.3 2.3 collective-permute-start.18
  93.8 7.8 %collective-permute-start.13 = (f32[4,16]{1,0:T(4,128)}, f32[4,16]{1,0:T(4,128)}, u32[]{:S(2)}, u32[]{:S(2)}) collective-permute-start(f32[4,16]{1,0:T(4,128)} %get-tuple-element.83), channel_id=1, source_target_pairs={{0,16},{8,24},{16,32},{24,40},{32,48},{40,56},{48,64},{56,72},{64,... | collective-permute-start | bytes 776 | tf_op jit(solution)/shard_map/ppermute | solution.py:19
  102.9 24.3 %collective-permute-done.13 = f32[4,16]{1,0:T(4,128)} collective-permute-done((f32[4,16]{1,0:T(4,128)}, f32[4,16]{1,0:T(4,128)}, u32[]{:S(2)}, u32[]{:S(2)}) %collective-permute-start.13) | collective-permute-done | bytes 288 | tf_op jit(solution)/shard_map/ppermute | solution.py:19
  128.4 6.8 %collective-permute-start.14 = (f32[4,16]{1,0:T(4,128)}, f32[4,16]{1,0:T(4,128)}, u32[]{:S(2)}, u32[]{:S(2)}) collective-permute-start(f32[4,16]{1,0:T(4,128)} %mul.469), channel_id=1, source_target_pairs={{0,32},{8,40},{16,48},{24,56},{32,64},{40,72},{48,80},{56,88},{64,... | collective-permute-start | bytes 776 | tf_op jit(solution)/shard_map/ppermute | solution.py:19
  139.1 8.3 %collective-permute-start.15 = (f32[4,16]{1,0:T(4,128)}, f32[4,16]{1,0:T(4,128)}, u32[]{:S(2)}, u32[]{:S(2)}) collective-permute-start(f32[4,16]{1,0:T(4,128)} %mul.470), channel_id=1, source_target_pairs={{0,64},{8,72},{16,80},{24,88},{32,96},{40,104},{48,112},{56,120},{... | collective-permute-start | bytes 776 | tf_op jit(solution)/shard_map/ppermute | solution.py:19
  150.7 8.0 %collective-permute-start.16 = (f32[4,16]{1,0:T(4,128)S(1)}, f32[4,16]{1,0:T(4,128)}, u32[]{:S(2)}, u32[]{:S(2)}) collective-permute-start(f32[4,16]{1,0:T(4,128)S(1)} %mul.471), channel_id=1, source_target_pairs={{0,8},{8,16},{16,24},{24,32},{32,40},{40,48},{48,56},{56,64},{64,7... | collective-permute-start | bytes 776 | tf_op jit(solution)/shard_map/ppermute | solution.py:19
  161.7 5.5 %collective-permute-start.19 = (f32[4,16,32,64]{3,2,1,0:T(8,128)S(1)}, f32[4,16,32,64]{3,2,1,0:T(8,128)S(1)}, u32[]{:S(2)}, u32[]{:S(2)}) collective-permute-start(f32[4,16,32,64]{3,2,1,0:T(8,128)S(1)} %multiply_add_fusion.3), channel_id=1, source_target_pairs={{0,32},{8,40},{16,48},{24,56},{32,64},{40,72},{48,80},{56,88},{64,... | collective-permute-start | bytes 1572872 | tf_op jit(solution)/shard_map/ppermute | solution.py:19
  170.8 18.9 %collective-permute-done.19 = f32[4,16,32,64]{3,2,1,0:T(8,128)S(1)} collective-permute-done((f32[4,16,32,64]{3,2,1,0:T(8,128)S(1)}, f32[4,16,32,64]{3,2,1,0:T(8,128)S(1)}, u32[]{:S(2)}, u32[]{:S(2)}) %collective-permute-start.19) | collective-permute-done | bytes 524320 | tf_op jit(solution)/shard_map/ppermute | solution.py:19
  190.6 7.2 %collective-permute-start.20 = (f32[4,16,32,64]{3,2,1,0:T(8,128)S(1)}, f32[4,16,32,64]{3,2,1,0:T(8,128)S(1)}, u32[]{:S(2)}, u32[]{:S(2)}) collective-permute-start(f32[4,16,32,64]{3,2,1,0:T(8,128)S(1)} %multiply_add_fusion.2), channel_id=1, source_target_pairs={{0,64},{8,72},{16,80},{24,88},{32,96},{40,104},{48,112},{56,120},{... | collective-permute-start | bytes 1572872 | tf_op jit(solution)/shard_map/ppermute | solution.py:19
  200.0 6.6 %fusion.4 = (f32[4,16,128]{2,1,0:T(8,128)}, f32[4,16,128]{2,1,0:T(8,128)}, f32[4,128,128]{1,2,0:T(8,128)S(1)}) fusion(f32[4,16,128]{2,1,0:T(8,128)S(1)} %copy-done.24, f32[4,128,128]{1,2,0:T(8,128)S(1)} %fusion.54, pred[128,128]{0,1:T(8,128)(4,1)S(1)} %copy-done.31, bf16[128,4,16,32]{0,3,2,1:T(8,128)(2,1)S(1)} %bitcast.135, ...), kind=kOutput, calls=%fused_computation.10 | convolution fusion | flops 412270592 | bytes 2244608 | tf_op jit(solution)/shard_map/ctgkp,csgkp->cgkts/dot_general | solution.py:101
  206.6 13.1 %collective-permute-done.20 = f32[4,16,32,64]{3,2,1,0:T(8,128)S(1)} collective-permute-done((f32[4,16,32,64]{3,2,1,0:T(8,128)S(1)}, f32[4,16,32,64]{3,2,1,0:T(8,128)S(1)}, u32[]{:S(2)}, u32[]{:S(2)}) %collective-permute-start.20) | collective-permute-done | bytes 524320 | tf_op jit(solution)/shard_map/ppermute | solution.py:19
  221.6 10.7 %collective-permute-start.21 = (f32[4,16,32,64]{3,2,1,0:T(8,128)}, f32[4,16,32,64]{3,2,1,0:T(8,128)}, u32[]{:S(2)}, u32[]{:S(2)}) collective-permute-start(f32[4,16,32,64]{3,2,1,0:T(8,128)} %multiply_add_fusion.1), channel_id=1, source_target_pairs={{0,136},{8,144},{16,152},{24,160},{32,168},{40,176},{48,184},{56,1... | collective-permute-start | bytes 1572872 | tf_op jit(solution)/shard_map/ppermute | solution.py:19
  234.2 12.7 %collective-permute-done.9 = f32[4,16,32,64]{3,2,1,0:T(8,128)S(1)} collective-permute-done((f32[4,16,32,64]{3,2,1,0:T(8,128)S(1)}, f32[4,16,32,64]{3,2,1,0:T(8,128)S(1)}, u32[]{:S(2)}, u32[]{:S(2)}) %collective-permute-start.9) | collective-permute-done | bytes 524320 | tf_op jit(solution)/shard_map/ppermute | solution.py:19
  250.1 3.0 collective-permute-start.11
  253.1 5.0 %fusion.11 = f32[1,128,4,16,32]{1,4,3,2,0:T(8,128)} fusion(bf16[128,4,16,32]{0,3,2,1:T(8,128)(2,1)S(1)} %bitcast.136, f32[4,16,128]{2,1,0:T(8,128)S(1)} %copy-done.24, f32[4,128,128]{1,2,0:T(8,128)S(1)} %fusion.54, pred[128,128]{0,1:T(8,128)(4,1)S(1)} %copy-done.31), kind=kOutput, calls=%fused_computation.17 | convolution fusion | flops 406847488 | bytes 1884160 | tf_op jit(solution)/shard_map/cgkts,ctgkp->csgkp/dot_general | solution.py:102
  266.4 41.0 %collective-permute-done.5 = f32[4,16]{1,0:T(4,128)} collective-permute-done((f32[4,16]{1,0:T(4,128)}, f32[4,16]{1,0:T(4,128)}, u32[]{:S(2)}, u32[]{:S(2)}) %collective-permute-start.5) | collective-permute-done | bytes 288 | tf_op jit(solution)/shard_map/ppermute | solution.py:19
  307.4 3.3 multiply_reduce_fusion.4
  310.7 1.9 fusion.27
  314.7 3.1 multiply_reduce_fusion.5
  317.7 4.2 multiply_reduce_fusion.3
  322.1 2.6 fusion.26
  326.8 106.5 %psum.7 = f32[12928]{0:T(1024)S(1)} all-reduce(f32[12928]{0:T(1024)S(1)} %concatenate.21), channel_id=1, replica_groups=mesh['ctx'=32,'fsdp'=8] {'ctx','fsdp'}, use_global_device_ids=true, to_apply=%region_18.19 | all-reduce | flops 12928 | bytes 103424 | tf_op jit(solution)/shard_map/psum | solution.py:162
  434.9 2.8 collective-permute-start.23
  439.1 2.7 collective-permute-done.23
  442.2 3.7 fusion.36
  (184 shorter events, 65.1 us)
Async XLA Ops:
  0.6 37.2 %copy-start.12 = (f32[1,128,64]{1,2,0:T(8,128)S(1)}, f32[1,128,64]{1,2,0:T(8,128)}, u32[]{:S(2)}) copy-start(f32[1,128,64]{1,2,0:T(8,128)} %param.10) | copy-start | bytes 98308
  0.6 37.4 %copy-start.8 = (bf16[1,128,2560]{2,1,0:T(8,128)(2,1)S(1)}, bf16[1,128,2560]{2,1,0:T(8,128)(2,1)}, u32[]{:S(2)}) copy-start(bf16[1,128,2560]{2,1,0:T(8,128)(2,1)} %param.9) | copy-start | bytes 1966084
  3.0 36.2 %copy-start.10 = (bf16[1,128,2048]{2,1,0:T(8,128)(2,1)S(1)}, bf16[1,128,2048]{2,1,0:T(8,128)(2,1)}, u32[]{:S(2)}) copy-start(bf16[1,128,2048]{2,1,0:T(8,128)(2,1)} %param.15) | copy-start | bytes 1572868
  3.1 34.9 %copy-start.6 = (f32[1,128,4,16]{3,2,1,0:T(4,128)}, f32[1,128,4,16]{3,2,1,0:T(4,128)S(1)}, u32[]{:S(2)}) copy-start(f32[1,128,4,16]{3,2,1,0:T(4,128)S(1)} %fusion.52) | copy-start | bytes 98308
  3.4 36.0 %copy-start.35 = (f32[4,16]{1,0:T(4,128)}, f32[4,16]{1,0:T(4,128)S(1)}, u32[]{:S(2)}) copy-start(f32[4,16]{1,0:T(4,128)S(1)} %exp.91) | copy-start | bytes 772
  3.4 36.0 %collective-permute-start.1 = (f32[4,16]{1,0:T(4,128)S(1)}, f32[4,16]{1,0:T(4,128)S(1)}, u32[]{:S(2)}, u32[]{:S(2)}) collective-permute-start(f32[4,16]{1,0:T(4,128)S(1)} %exp.91), channel_id=1, source_target_pairs={{8,0},{16,8},{24,16},{32,24},{40,32},{48,40},{56,48},{64,56},{72,6... | collective-permute-start | bytes 776 | tf_op jit(solution)/shard_map/ppermute | solution.py:19
  8.5 30.9 %collective-permute-start.12 = (f32[4,16]{1,0:T(4,128)S(1)}, f32[4,16]{1,0:T(4,128)S(1)}, u32[]{:S(2)}, u32[]{:S(2)}) collective-permute-start(f32[4,16]{1,0:T(4,128)S(1)} %exp.91), channel_id=1, source_target_pairs={{0,8},{8,16},{16,24},{24,32},{32,40},{40,48},{48,56},{56,64},{64,7... | collective-permute-start | bytes 776 | tf_op jit(solution)/shard_map/ppermute | solution.py:19
  12.4 27.7 %collective-permute-start = (bf16[3,2560]{1,0:T(4,128)(2,1)S(1)}, bf16[3,2560]{1,0:T(4,128)(2,1)S(1)}, u32[]{:S(2)}, u32[]{:S(2)}) collective-permute-start(bf16[3,2560]{1,0:T(4,128)(2,1)S(1)} %slice_bitcast_fusion), channel_id=1, source_target_pairs={{0,8},{8,16},{16,24},{24,32},{32,40},{40,48},{48,56},{56,64},{64,7... | collective-permute-start | bytes 46088 | tf_op jit(solution)/shard_map/ppermute | solution.py:19
  49.1 34.5 %collective-permute-start.17 = (f32[4,16,32,64]{3,2,1,0:T(8,128)S(1)}, f32[4,16,32,64]{3,2,1,0:T(8,128)S(1)}, u32[]{:S(2)}, u32[]{:S(2)}) collective-permute-start(f32[4,16,32,64]{3,2,1,0:T(8,128)S(1)} %convolution_add_fusion), channel_id=1, source_target_pairs={{0,8},{8,16},{16,24},{24,32},{32,40},{40,48},{48,56},{56,64},{64,7... | collective-permute-start | bytes 1572872 | tf_op jit(solution)/shard_map/ppermute | solution.py:19
  61.8 21.9 %collective-permute-start.6 = (f32[4,16,32,64]{3,2,1,0:T(8,128)S(1)}, f32[4,16,32,64]{3,2,1,0:T(8,128)S(1)}, u32[]{:S(2)}, u32[]{:S(2)}) collective-permute-start(f32[4,16,32,64]{3,2,1,0:T(8,128)S(1)} %convolution_add_fusion.1), channel_id=1, source_target_pairs={{8,0},{16,8},{24,16},{32,24},{40,32},{48,40},{56,48},{64,56},{72,6... | collective-permute-start | bytes 1572872 | tf_op jit(solution)/shard_map/ppermute | solution.py:19
  85.3 74.7 %collective-permute-start.18 = (f32[4,16,32,64]{3,2,1,0:T(8,128)}, f32[4,16,32,64]{3,2,1,0:T(8,128)}, u32[]{:S(2)}, u32[]{:S(2)}) collective-permute-start(f32[4,16,32,64]{3,2,1,0:T(8,128)} %get-tuple-element.86), channel_id=1, source_target_pairs={{0,16},{8,24},{16,32},{24,40},{32,48},{40,56},{48,64},{56,72},{64,... | collective-permute-start | bytes 1572872 | tf_op jit(solution)/shard_map/ppermute | solution.py:19
  87.6 79.6 %collective-permute-start.7 = (f32[4,16,32,64]{3,2,1,0:T(8,128)}, f32[4,16,32,64]{3,2,1,0:T(8,128)}, u32[]{:S(2)}, u32[]{:S(2)}) collective-permute-start(f32[4,16,32,64]{3,2,1,0:T(8,128)} %get-tuple-element.87), channel_id=1, source_target_pairs={{16,0},{24,8},{32,16},{40,24},{48,32},{56,40},{64,48},{72,56},{80,... | collective-permute-start | bytes 1572872 | tf_op jit(solution)/shard_map/ppermute | solution.py:19
  93.8 33.4 %collective-permute-start.13 = (f32[4,16]{1,0:T(4,128)}, f32[4,16]{1,0:T(4,128)}, u32[]{:S(2)}, u32[]{:S(2)}) collective-permute-start(f32[4,16]{1,0:T(4,128)} %get-tuple-element.83), channel_id=1, source_target_pairs={{0,16},{8,24},{16,32},{24,40},{32,48},{40,56},{48,64},{56,72},{64,... | collective-permute-start | bytes 776 | tf_op jit(solution)/shard_map/ppermute | solution.py:19
  101.6 33.7 %collective-permute-start.2 = (f32[4,16]{1,0:T(4,128)}, f32[4,16]{1,0:T(4,128)}, u32[]{:S(2)}, u32[]{:S(2)}) collective-permute-start(f32[4,16]{1,0:T(4,128)} %get-tuple-element.84), channel_id=1, source_target_pairs={{16,0},{24,8},{32,16},{40,24},{48,32},{56,40},{64,48},{72,56},{80,... | collective-permute-start | bytes 776 | tf_op jit(solution)/shard_map/ppermute | solution.py:19
  128.4 9.4 %collective-permute-start.14 = (f32[4,16]{1,0:T(4,128)}, f32[4,16]{1,0:T(4,128)}, u32[]{:S(2)}, u32[]{:S(2)}) collective-permute-start(f32[4,16]{1,0:T(4,128)} %mul.469), channel_id=1, source_target_pairs={{0,32},{8,40},{16,48},{24,56},{32,64},{40,72},{48,80},{56,88},{64,... | collective-permute-start | bytes 776 | tf_op jit(solution)/shard_map/ppermute | solution.py:19
  136.5 10.9 %collective-permute-start.3 = (f32[4,16]{1,0:T(4,128)}, f32[4,16]{1,0:T(4,128)}, u32[]{:S(2)}, u32[]{:S(2)}) collective-permute-start(f32[4,16]{1,0:T(4,128)} %mul.440), channel_id=1, source_target_pairs={{32,0},{40,8},{48,16},{56,24},{64,32},{72,40},{80,48},{88,56},{96,... | collective-permute-start | bytes 776 | tf_op jit(solution)/shard_map/ppermute | solution.py:19
  139.1 10.9 %collective-permute-start.15 = (f32[4,16]{1,0:T(4,128)}, f32[4,16]{1,0:T(4,128)}, u32[]{:S(2)}, u32[]{:S(2)}) collective-permute-start(f32[4,16]{1,0:T(4,128)} %mul.470), channel_id=1, source_target_pairs={{0,64},{8,72},{16,80},{24,88},{32,96},{40,104},{48,112},{56,120},{... | collective-permute-start | bytes 776 | tf_op jit(solution)/shard_map/ppermute | solution.py:19
  148.7 10.0 %collective-permute-start.4 = (f32[4,16]{1,0:T(4,128)}, f32[4,16]{1,0:T(4,128)}, u32[]{:S(2)}, u32[]{:S(2)}) collective-permute-start(f32[4,16]{1,0:T(4,128)} %mul.441), channel_id=1, source_target_pairs={{64,0},{72,8},{80,16},{88,24},{96,32},{104,40},{112,48},{120,56},{... | collective-permute-start | bytes 776 | tf_op jit(solution)/shard_map/ppermute | solution.py:19
  150.7 109.7 %collective-permute-start.16 = (f32[4,16]{1,0:T(4,128)S(1)}, f32[4,16]{1,0:T(4,128)}, u32[]{:S(2)}, u32[]{:S(2)}) collective-permute-start(f32[4,16]{1,0:T(4,128)S(1)} %mul.471), channel_id=1, source_target_pairs={{0,8},{8,16},{16,24},{24,32},{32,40},{40,48},{48,56},{56,64},{64,7... | collective-permute-start | bytes 776 | tf_op jit(solution)/shard_map/ppermute | solution.py:19
  161.7 28.1 %collective-permute-start.19 = (f32[4,16,32,64]{3,2,1,0:T(8,128)S(1)}, f32[4,16,32,64]{3,2,1,0:T(8,128)S(1)}, u32[]{:S(2)}, u32[]{:S(2)}) collective-permute-start(f32[4,16,32,64]{3,2,1,0:T(8,128)S(1)} %multiply_add_fusion.3), channel_id=1, source_target_pairs={{0,32},{8,40},{16,48},{24,56},{32,64},{40,72},{48,80},{56,88},{64,... | collective-permute-start | bytes 1572872 | tf_op jit(solution)/shard_map/ppermute | solution.py:19
  168.9 28.9 %collective-permute-start.8 = (f32[4,16,32,64]{3,2,1,0:T(8,128)S(1)}, f32[4,16,32,64]{3,2,1,0:T(8,128)S(1)}, u32[]{:S(2)}, u32[]{:S(2)}) collective-permute-start(f32[4,16,32,64]{3,2,1,0:T(8,128)S(1)} %multiply_add_fusion.10), channel_id=1, source_target_pairs={{32,0},{40,8},{48,16},{56,24},{64,32},{72,40},{80,48},{88,56},{96,... | collective-permute-start | bytes 1572872 | tf_op jit(solution)/shard_map/ppermute | solution.py:19
  190.6 29.1 %collective-permute-start.20 = (f32[4,16,32,64]{3,2,1,0:T(8,128)S(1)}, f32[4,16,32,64]{3,2,1,0:T(8,128)S(1)}, u32[]{:S(2)}, u32[]{:S(2)}) collective-permute-start(f32[4,16,32,64]{3,2,1,0:T(8,128)S(1)} %multiply_add_fusion.2), channel_id=1, source_target_pairs={{0,64},{8,72},{16,80},{24,88},{32,96},{40,104},{48,112},{56,120},{... | collective-permute-start | bytes 1572872 | tf_op jit(solution)/shard_map/ppermute | solution.py:19
  198.7 48.2 %collective-permute-start.9 = (f32[4,16,32,64]{3,2,1,0:T(8,128)S(1)}, f32[4,16,32,64]{3,2,1,0:T(8,128)S(1)}, u32[]{:S(2)}, u32[]{:S(2)}) collective-permute-start(f32[4,16,32,64]{3,2,1,0:T(8,128)S(1)} %multiply_add_fusion.9), channel_id=1, source_target_pairs={{64,0},{72,8},{80,16},{88,24},{96,32},{104,40},{112,48},{120,56},{... | collective-permute-start | bytes 1572872 | tf_op jit(solution)/shard_map/ppermute | solution.py:19
  221.6 85.8 %collective-permute-start.21 = (f32[4,16,32,64]{3,2,1,0:T(8,128)}, f32[4,16,32,64]{3,2,1,0:T(8,128)}, u32[]{:S(2)}, u32[]{:S(2)}) collective-permute-start(f32[4,16,32,64]{3,2,1,0:T(8,128)} %multiply_add_fusion.1), channel_id=1, source_target_pairs={{0,136},{8,144},{16,152},{24,160},{32,168},{40,176},{48,184},{56,1... | collective-permute-start | bytes 1572872 | tf_op jit(solution)/shard_map/ppermute | solution.py:19
  232.2 75.1 %collective-permute-start.22 = (f32[4,16,32,64]{3,2,1,0:T(8,128)}, f32[4,16,32,64]{3,2,1,0:T(8,128)}, u32[]{:S(2)}, u32[]{:S(2)}) collective-permute-start(f32[4,16,32,64]{3,2,1,0:T(8,128)} %multiply_add_fusion.1), channel_id=1, source_target_pairs={{0,8},{8,16},{16,24},{24,32},{32,40},{40,48},{48,56},{56,64},{64,7... | collective-permute-start | bytes 1572872 | tf_op jit(solution)/shard_map/ppermute | solution.py:19
  248.8 58.6 %collective-permute-start.10 = (f32[4,16,32,64]{3,2,1,0:T(8,128)}, f32[4,16,32,64]{3,2,1,0:T(8,128)}, u32[]{:S(2)}, u32[]{:S(2)}) collective-permute-start(f32[4,16,32,64]{3,2,1,0:T(8,128)} %multiply_add_fusion.8), channel_id=1, source_target_pairs={{136,0},{144,8},{152,16},{160,24},{168,32},{176,40},{184,48},{192,... | collective-permute-start | bytes 1572872 | tf_op jit(solution)/shard_map/ppermute | solution.py:19
  250.1 57.3 %collective-permute-start.11 = (f32[4,16,32,64]{3,2,1,0:T(8,128)}, f32[4,16,32,64]{3,2,1,0:T(8,128)}, u32[]{:S(2)}, u32[]{:S(2)}) collective-permute-start(f32[4,16,32,64]{3,2,1,0:T(8,128)} %multiply_add_fusion.8), channel_id=1, source_target_pairs={{8,0},{16,8},{24,16},{32,24},{40,32},{48,40},{56,48},{64,56},{72,6... | collective-permute-start | bytes 1572872 | tf_op jit(solution)/shard_map/ppermute | solution.py:19
  260.4 47.0 %collective-permute-start.5 = (f32[4,16]{1,0:T(4,128)}, f32[4,16]{1,0:T(4,128)}, u32[]{:S(2)}, u32[]{:S(2)}) collective-permute-start(f32[4,16]{1,0:T(4,128)} %mul.442), channel_id=1, source_target_pairs={{8,0},{16,8},{24,16},{32,24},{40,32},{48,40},{56,48},{64,56},{72,6... | collective-permute-start | bytes 776 | tf_op jit(solution)/shard_map/ppermute | solution.py:19
  266.4 44.4 %copy-start.2 = (f32[128,2048]{0,1:T(8,128)S(1)}, f32[128,2048]{0,1:T(8,128)}, u32[]{:S(2)}) copy-start(f32[128,2048]{0,1:T(8,128)} %copy-done) | copy-start | bytes 3145732
  266.4 44.4 %copy-start.11 = (f32[4,64,128]{2,1,0:T(8,128)S(1)}, f32[4,64,128]{2,1,0:T(8,128)}, u32[]{:S(2)}) copy-start(f32[4,64,128]{2,1,0:T(8,128)} %fusion.55) | copy-start | bytes 393220
  324.8 109.8 %copy-start.3 = (f32[128,2560]{0,1:T(8,128)S(1)}, f32[128,2560]{0,1:T(8,128)}, u32[]{:S(2)}) copy-start(f32[128,2560]{0,1:T(8,128)} %get-tuple-element.63) | copy-start | bytes 3932164
  434.9 6.8 %collective-permute-start.23 = (f32[3,2560]{1,0:T(4,128)S(1)}, f32[3,2560]{1,0:T(4,128)S(1)}, u32[]{:S(2)}, u32[]{:S(2)}) collective-permute-start(f32[3,2560]{1,0:T(4,128)S(1)} %copy.147), channel_id=1, source_target_pairs={{8,0},{16,8},{24,16},{32,24},{40,32},{48,40},{56,48},{64,56},{72,6... | collective-permute-start | bytes 92168 | tf_op jit(solution)/shard_map/ppermute | solution.py:19
  (32 other events, 214.2 us)
where the time goes:
time: 449 us; the launch traced here: 447 us
  waiting for transfers between devices  133 us (30%)
  blocking collectives  129 us (29%)
  starting transfers between devices  99.2 us (22%)
  other arithmetic  44.1 us (10%)
  matrix products  26.2 us (6%)
  local copies, waits for them, and re-layouts  14.5 us (3%)
    ppermute x24, waiting for transfers between devices, from_behind(): return lax.ppermute(value, axis, pairs)  133 us
    psum x1, blocking collectives, body(): packed = lax.psum(packed, ('ctx', 'fsdp'))  107 us
    ppermute x24, starting transfers between devices, from_behind(): return lax.ppermute(value, axis, pairs)  99.2 us
    all_gather x1, blocking collectives, body(): lax.all_gather(jnp.concatenate([conv_weight, conv_bias[None]], 0), 'fsdp'...  22.3 us
    add x7, other arithmetic, compose(): later[0][..., None, None] * earlier[1] + later[1]  10.5 us
  transfers between devices with their start and end apart: 24, of which 7 were waited for; matrix products, arithmetic and copies ran while one was open for 10% of the time, Pallas kernels for 0%

commit v1 on v0

--- a/solution.py
+++ b/solution.py
@@ -46,8 +46,16 @@
     per_group = HW // GW
     inner_width = HW * P_SIZE
     blocks = tok_rows // SPAN
-    params_all = lax.all_gather(
-        jnp.concatenate([conv_weight, conv_bias[None]], 0), "fsdp", axis=1, tiled=True
+    params_all = jnp.concatenate(
+        lax.all_to_all(
+            jnp.stack(
+                lax.axis_size("fsdp") * [jnp.concatenate([conv_weight, conv_bias[None]], 0)], axis=0
+            ),
+            "fsdp",
+            0,
+            0,
+        ),
+        axis=1,
     ).astype(jnp.float32)
     weight_f = params_all[:KW]
     bias_f = params_all[KW]

time: 449 us -> 430 us (0.958)
  blocking collectives: 129 us -> 107 us
    all_gather x1 -> x0, blocking collectives: 22.3 us -> none  [body(): lax.all_gather(jnp.concatenate([conv_weight, conv_bias[None]], 0), 'fsdp'...]
    all_to_all x0 -> x1, starting transfers between devices: none -> 4.8 us  [body(): lax.all_to_all(jnp.stack(lax.axis_size('fsdp') * [jnp.concatenate([conv_w...]
  transfers between devices with their start and end apart: 24 -> 25, of which waited for: 7 -> 8; matrix products, arithmetic and copies ran while one was open for 10% -> 12% of each run, Pallas kernels for 0% -> 0%
where the time goes in v1:
time: 430 us; the launch traced here: 428 us
  waiting for transfers between devices  132 us (31%)
  blocking collectives  107 us (25%)
  starting transfers between devices  102 us (24%)
  other arithmetic  44.7 us (10%)
  matrix products  26.2 us (6%)
  local copies, waits for them, and re-layouts  15.3 us (4%)
    ppermute x24, waiting for transfers between devices, from_behind(): return lax.ppermute(value, axis, pairs)  132 us
    psum x1, blocking collectives, body(): packed = lax.psum(packed, ('ctx', 'fsdp'))  107 us
    ppermute x24, starting transfers between devices, from_behind(): return lax.ppermute(value, axis, pairs)  96.9 us
    add x7, other arithmetic, compose(): later[0][..., None, None] * earlier[1] + later[1]  10.5 us
  transfers between devices with their start and end apart: 25, of which 8 were waited for; matrix products, arithmetic and copies ran while one was open for 12% of the time, Pallas kernels for 0%

profile of v1, /device:TPU:1, one launch (start us, length us, event | category | flops | bytes accessed | tf_op | source)
XLA Modules:
  0.0 428.1 jit_solution(7634683368839689635)
XLA Ops:
  3.4 5.1 %collective-permute-start.1 = (f32[4,16]{1,0:T(4,128)S(1)}, f32[4,16]{1,0:T(4,128)S(1)}, u32[]{:S(2)}, u32[]{:S(2)}) collective-permute-start(f32[4,16]{1,0:T(4,128)S(1)} %exp.91), channel_id=1, source_target_pairs={{8,0},{16,8},{24,16},{32,24},{40,32},{48,40},{56,48},{64,56},{72,6... | collective-permute-start | bytes 776 | tf_op jit(solution)/shard_map/ppermute | solution.py:19
  8.5 3.0 collective-permute-start.12
  13.6 4.8 %all-to-all-start = ((bf16[8,5,320]{2,1,0:T(8,128)(2,1)}), bf16[8,5,320]{2,1,0:T(8,128)(2,1)S(1)}, u32[]{:S(2)}, u32[]{:S(2)}) async-start(bf16[8,5,320]{2,1,0:T(8,128)(2,1)} %stack.12), calls=%async_computation | async-start | bytes 98304 | tf_op jit(solution)/shard_map/all_to_all | solution.py:50
  18.4 2.8 collective-permute-start
  27.4 3.9 fusion.25
  33.4 4.9 %collective-permute-start.17 = (f32[4,16,32,64]{3,2,1,0:T(8,128)S(1)}, f32[4,16,32,64]{3,2,1,0:T(8,128)S(1)}, u32[]{:S(2)}, u32[]{:S(2)}) collective-permute-start(f32[4,16,32,64]{3,2,1,0:T(8,128)S(1)} %convolution_add_fusion), channel_id=1, source_target_pairs={{0,8},{8,16},{16,24},{24,32},{32,40},{40,48},{48,56},{56,64},{64,7... | collective-permute-start | bytes 1572872 | tf_op jit(solution)/shard_map/ppermute | solution.py:19
  41.4 19.9 %collective-permute-done.17 = f32[4,16,32,64]{3,2,1,0:T(8,128)S(1)} collective-permute-done((f32[4,16,32,64]{3,2,1,0:T(8,128)S(1)}, f32[4,16,32,64]{3,2,1,0:T(8,128)S(1)}, u32[]{:S(2)}, u32[]{:S(2)}) %collective-permute-start.17) | collective-permute-done | bytes 524320 | tf_op jit(solution)/shard_map/ppermute | solution.py:19
  62.9 2.3 collective-permute-start.18
  71.5 9.6 %collective-permute-start.13 = (f32[4,16]{1,0:T(4,128)}, f32[4,16]{1,0:T(4,128)}, u32[]{:S(2)}, u32[]{:S(2)}) collective-permute-start(f32[4,16]{1,0:T(4,128)} %get-tuple-element.83), channel_id=1, source_target_pairs={{0,16},{8,24},{16,32},{24,40},{32,48},{40,56},{48,64},{56,72},{64,... | collective-permute-start | bytes 776 | tf_op jit(solution)/shard_map/ppermute | solution.py:19
  82.3 22.5 %collective-permute-done.13 = f32[4,16]{1,0:T(4,128)} collective-permute-done((f32[4,16]{1,0:T(4,128)}, f32[4,16]{1,0:T(4,128)}, u32[]{:S(2)}, u32[]{:S(2)}) %collective-permute-start.13) | collective-permute-done | bytes 288 | tf_op jit(solution)/shard_map/ppermute | solution.py:19
  106.1 10.4 %collective-permute-start.14 = (f32[4,16]{1,0:T(4,128)}, f32[4,16]{1,0:T(4,128)}, u32[]{:S(2)}, u32[]{:S(2)}) collective-permute-start(f32[4,16]{1,0:T(4,128)} %mul.469), channel_id=1, source_target_pairs={{0,32},{8,40},{16,48},{24,56},{32,64},{40,72},{48,80},{56,88},{64,... | collective-permute-start | bytes 776 | tf_op jit(solution)/shard_map/ppermute | solution.py:19
  120.4 5.3 %collective-permute-start.15 = (f32[4,16]{1,0:T(4,128)}, f32[4,16]{1,0:T(4,128)}, u32[]{:S(2)}, u32[]{:S(2)}) collective-permute-start(f32[4,16]{1,0:T(4,128)} %mul.470), channel_id=1, source_target_pairs={{0,64},{8,72},{16,80},{24,88},{32,96},{40,104},{48,112},{56,120},{... | collective-permute-start | bytes 776 | tf_op jit(solution)/shard_map/ppermute | solution.py:19
  129.0 9.1 %collective-permute-start.16 = (f32[4,16]{1,0:T(4,128)S(1)}, f32[4,16]{1,0:T(4,128)}, u32[]{:S(2)}, u32[]{:S(2)}) collective-permute-start(f32[4,16]{1,0:T(4,128)S(1)} %mul.471), channel_id=1, source_target_pairs={{0,8},{8,16},{16,24},{24,32},{32,40},{40,48},{48,56},{56,64},{64,7... | collective-permute-start | bytes 776 | tf_op jit(solution)/shard_map/ppermute | solution.py:19
  142.0 5.9 %collective-permute-start.19 = (f32[4,16,32,64]{3,2,1,0:T(8,128)S(1)}, f32[4,16,32,64]{3,2,1,0:T(8,128)S(1)}, u32[]{:S(2)}, u32[]{:S(2)}) collective-permute-start(f32[4,16,32,64]{3,2,1,0:T(8,128)S(1)} %multiply_add_fusion.3), channel_id=1, source_target_pairs={{0,32},{8,40},{16,48},{24,56},{32,64},{40,72},{48,80},{56,88},{64,... | collective-permute-start | bytes 1572872 | tf_op jit(solution)/shard_map/ppermute | solution.py:19
  151.5 18.9 %collective-permute-done.19 = f32[4,16,32,64]{3,2,1,0:T(8,128)S(1)} collective-permute-done((f32[4,16,32,64]{3,2,1,0:T(8,128)S(1)}, f32[4,16,32,64]{3,2,1,0:T(8,128)S(1)}, u32[]{:S(2)}, u32[]{:S(2)}) %collective-permute-start.19) | collective-permute-done | bytes 524320 | tf_op jit(solution)/shard_map/ppermute | solution.py:19
  171.3 7.2 %collective-permute-start.20 = (f32[4,16,32,64]{3,2,1,0:T(8,128)S(1)}, f32[4,16,32,64]{3,2,1,0:T(8,128)S(1)}, u32[]{:S(2)}, u32[]{:S(2)}) collective-permute-start(f32[4,16,32,64]{3,2,1,0:T(8,128)S(1)} %multiply_add_fusion.2), channel_id=1, source_target_pairs={{0,64},{8,72},{16,80},{24,88},{32,96},{40,104},{48,112},{56,120},{... | collective-permute-start | bytes 1572872 | tf_op jit(solution)/shard_map/ppermute | solution.py:19
  180.7 6.6 %fusion.4 = (f32[4,16,128]{2,1,0:T(8,128)}, f32[4,16,128]{2,1,0:T(8,128)}, f32[4,128,128]{1,2,0:T(8,128)S(1)}) fusion(f32[4,16,128]{2,1,0:T(8,128)S(1)} %copy-done.24, f32[4,128,128]{1,2,0:T(8,128)S(1)} %fusion.54, pred[128,128]{0,1:T(8,128)(4,1)S(1)} %copy-done.31, bf16[128,4,16,32]{0,3,2,1:T(8,128)(2,1)S(1)} %bitcast.130, ...), kind=kOutput, calls=%fused_computation.10 | convolution fusion | flops 412270592 | bytes 2244608 | tf_op jit(solution)/shard_map/ctgkp,csgkp->cgkts/dot_general | solution.py:109
  187.3 13.1 %collective-permute-done.20 = f32[4,16,32,64]{3,2,1,0:T(8,128)S(1)} collective-permute-done((f32[4,16,32,64]{3,2,1,0:T(8,128)S(1)}, f32[4,16,32,64]{3,2,1,0:T(8,128)S(1)}, u32[]{:S(2)}, u32[]{:S(2)}) %collective-permute-start.20) | collective-permute-done | bytes 524320 | tf_op jit(solution)/shard_map/ppermute | solution.py:19
  202.2 10.7 %collective-permute-start.21 = (f32[4,16,32,64]{3,2,1,0:T(8,128)}, f32[4,16,32,64]{3,2,1,0:T(8,128)}, u32[]{:S(2)}, u32[]{:S(2)}) collective-permute-start(f32[4,16,32,64]{3,2,1,0:T(8,128)} %multiply_add_fusion.1), channel_id=1, source_target_pairs={{0,136},{8,144},{16,152},{24,160},{32,168},{40,176},{48,184},{56,1... | collective-permute-start | bytes 1572872 | tf_op jit(solution)/shard_map/ppermute | solution.py:19
  214.8 12.6 %collective-permute-done.9 = f32[4,16,32,64]{3,2,1,0:T(8,128)S(1)} collective-permute-done((f32[4,16,32,64]{3,2,1,0:T(8,128)S(1)}, f32[4,16,32,64]{3,2,1,0:T(8,128)S(1)}, u32[]{:S(2)}, u32[]{:S(2)}) %collective-permute-start.9) | collective-permute-done | bytes 524320 | tf_op jit(solution)/shard_map/ppermute | solution.py:19
  230.6 3.0 collective-permute-start.11
  233.6 5.0 %fusion.11 = f32[1,128,4,16,32]{1,4,3,2,0:T(8,128)} fusion(bf16[128,4,16,32]{0,3,2,1:T(8,128)(2,1)S(1)} %bitcast.131, f32[4,16,128]{2,1,0:T(8,128)S(1)} %copy-done.24, f32[4,128,128]{1,2,0:T(8,128)S(1)} %fusion.54, pred[128,128]{0,1:T(8,128)(4,1)S(1)} %copy-done.31), kind=kOutput, calls=%fused_computation.17 | convolution fusion | flops 406847488 | bytes 1884160 | tf_op jit(solution)/shard_map/cgkts,ctgkp->csgkp/dot_general | solution.py:110
  246.9 41.2 %collective-permute-done.5 = f32[4,16]{1,0:T(4,128)} collective-permute-done((f32[4,16]{1,0:T(4,128)}, f32[4,16]{1,0:T(4,128)}, u32[]{:S(2)}, u32[]{:S(2)}) %collective-permute-start.5) | collective-permute-done | bytes 288 | tf_op jit(solution)/shard_map/ppermute | solution.py:19
  288.1 3.3 multiply_reduce_fusion.4
  291.4 1.9 fusion.27
  295.3 3.1 multiply_reduce_fusion.5
  298.4 4.2 multiply_reduce_fusion.3
  302.8 2.6 fusion.26
  307.4 106.9 %psum.7 = f32[12928]{0:T(1024)S(1)} all-reduce(f32[12928]{0:T(1024)S(1)} %concatenate.21), channel_id=1, replica_groups=mesh['ctx'=32,'fsdp'=8] {'ctx','fsdp'}, use_global_device_ids=true, to_apply=%region_18.19 | all-reduce | flops 12928 | bytes 103424 | tf_op jit(solution)/shard_map/psum | solution.py:170
  416.0 2.9 collective-permute-start.23
  420.2 2.6 collective-permute-done.23
  423.3 3.7 fusion.36
  (186 shorter events, 67.6 us)
Async XLA Ops:
  0.6 21.2 %copy-start.12 = (f32[1,128,64]{1,2,0:T(8,128)S(1)}, f32[1,128,64]{1,2,0:T(8,128)}, u32[]{:S(2)}) copy-start(f32[1,128,64]{1,2,0:T(8,128)} %param.10) | copy-start | bytes 98308
  3.0 20.0 %copy-start.10 = (bf16[1,128,2048]{2,1,0:T(8,128)(2,1)S(1)}, bf16[1,128,2048]{2,1,0:T(8,128)(2,1)}, u32[]{:S(2)}) copy-start(bf16[1,128,2048]{2,1,0:T(8,128)(2,1)} %param.15) | copy-start | bytes 1572868
  3.4 19.8 %copy-start.35 = (f32[4,16]{1,0:T(4,128)}, f32[4,16]{1,0:T(4,128)S(1)}, u32[]{:S(2)}) copy-start(f32[4,16]{1,0:T(4,128)S(1)} %exp.91) | copy-start | bytes 772
  3.4 19.8 %collective-permute-start.1 = (f32[4,16]{1,0:T(4,128)S(1)}, f32[4,16]{1,0:T(4,128)S(1)}, u32[]{:S(2)}, u32[]{:S(2)}) collective-permute-start(f32[4,16]{1,0:T(4,128)S(1)} %exp.91), channel_id=1, source_target_pairs={{8,0},{16,8},{24,16},{32,24},{40,32},{48,40},{56,48},{64,56},{72,6... | collective-permute-start | bytes 776 | tf_op jit(solution)/shard_map/ppermute | solution.py:19
  8.5 14.7 %collective-permute-start.12 = (f32[4,16]{1,0:T(4,128)S(1)}, f32[4,16]{1,0:T(4,128)S(1)}, u32[]{:S(2)}, u32[]{:S(2)}) collective-permute-start(f32[4,16]{1,0:T(4,128)S(1)} %exp.91), channel_id=1, source_target_pairs={{0,8},{8,16},{16,24},{24,32},{32,40},{40,48},{48,56},{56,64},{64,7... | collective-permute-start | bytes 776 | tf_op jit(solution)/shard_map/ppermute | solution.py:19
  13.6 13.2 %all-to-all-start = ((bf16[8,5,320]{2,1,0:T(8,128)(2,1)}), bf16[8,5,320]{2,1,0:T(8,128)(2,1)S(1)}, u32[]{:S(2)}, u32[]{:S(2)}) async-start(bf16[8,5,320]{2,1,0:T(8,128)(2,1)} %stack.12), calls=%async_computation | async-start | bytes 98304 | tf_op jit(solution)/shard_map/all_to_all | solution.py:50
  18.4 5.5 %collective-permute-start = (bf16[3,2560]{1,0:T(4,128)(2,1)S(1)}, bf16[3,2560]{1,0:T(4,128)(2,1)S(1)}, u32[]{:S(2)}, u32[]{:S(2)}) collective-permute-start(bf16[3,2560]{1,0:T(4,128)(2,1)S(1)} %slice_bitcast_fusion), channel_id=1, source_target_pairs={{0,8},{8,16},{16,24},{24,32},{32,40},{40,48},{48,56},{56,64},{64,7... | collective-permute-start | bytes 46088 | tf_op jit(solution)/shard_map/ppermute | solution.py:19
  33.4 27.9 %copy-start.36 = (f32[4,16]{1,0:T(4,128)S(1)}, f32[4,16]{1,0:T(4,128)}, u32[]{:S(2)}) copy-start(f32[4,16]{1,0:T(4,128)} %copy-done.35) | copy-start | bytes 772
  33.4 27.9 %collective-permute-start.17 = (f32[4,16,32,64]{3,2,1,0:T(8,128)S(1)}, f32[4,16,32,64]{3,2,1,0:T(8,128)S(1)}, u32[]{:S(2)}, u32[]{:S(2)}) collective-permute-start(f32[4,16,32,64]{3,2,1,0:T(8,128)S(1)} %convolution_add_fusion), channel_id=1, source_target_pairs={{0,8},{8,16},{16,24},{24,32},{32,40},{40,48},{48,56},{56,64},{64,7... | collective-permute-start | bytes 1572872 | tf_op jit(solution)/shard_map/ppermute | solution.py:19
  39.4 21.9 %collective-permute-start.6 = (f32[4,16,32,64]{3,2,1,0:T(8,128)S(1)}, f32[4,16,32,64]{3,2,1,0:T(8,128)S(1)}, u32[]{:S(2)}, u32[]{:S(2)}) collective-permute-start(f32[4,16,32,64]{3,2,1,0:T(8,128)S(1)} %convolution_add_fusion.1), channel_id=1, source_target_pairs={{8,0},{16,8},{24,16},{32,24},{40,32},{48,40},{56,48},{64,56},{72,6... | collective-permute-start | bytes 1572872 | tf_op jit(solution)/shard_map/ppermute | solution.py:19
  62.9 77.4 %collective-permute-start.18 = (f32[4,16,32,64]{3,2,1,0:T(8,128)}, f32[4,16,32,64]{3,2,1,0:T(8,128)}, u32[]{:S(2)}, u32[]{:S(2)}) collective-permute-start(f32[4,16,32,64]{3,2,1,0:T(8,128)} %get-tuple-element.86), channel_id=1, source_target_pairs={{0,16},{8,24},{16,32},{24,40},{32,48},{40,56},{48,64},{56,72},{64,... | collective-permute-start | bytes 1572872 | tf_op jit(solution)/shard_map/ppermute | solution.py:19
  65.2 82.7 %collective-permute-start.7 = (f32[4,16,32,64]{3,2,1,0:T(8,128)}, f32[4,16,32,64]{3,2,1,0:T(8,128)}, u32[]{:S(2)}, u32[]{:S(2)}) collective-permute-start(f32[4,16,32,64]{3,2,1,0:T(8,128)} %get-tuple-element.87), channel_id=1, source_target_pairs={{16,0},{24,8},{32,16},{40,24},{48,32},{56,40},{64,48},{72,56},{80,... | collective-permute-start | bytes 1572872 | tf_op jit(solution)/shard_map/ppermute | solution.py:19
  71.5 33.4 %collective-permute-start.13 = (f32[4,16]{1,0:T(4,128)}, f32[4,16]{1,0:T(4,128)}, u32[]{:S(2)}, u32[]{:S(2)}) collective-permute-start(f32[4,16]{1,0:T(4,128)} %get-tuple-element.83), channel_id=1, source_target_pairs={{0,16},{8,24},{16,32},{24,40},{32,48},{40,56},{48,64},{56,72},{64,... | collective-permute-start | bytes 776 | tf_op jit(solution)/shard_map/ppermute | solution.py:19
  81.0 35.5 %collective-permute-start.2 = (f32[4,16]{1,0:T(4,128)}, f32[4,16]{1,0:T(4,128)}, u32[]{:S(2)}, u32[]{:S(2)}) collective-permute-start(f32[4,16]{1,0:T(4,128)} %get-tuple-element.84), channel_id=1, source_target_pairs={{16,0},{24,8},{32,16},{40,24},{48,32},{56,40},{64,48},{72,56},{80,... | collective-permute-start | bytes 776 | tf_op jit(solution)/shard_map/ppermute | solution.py:19
  106.1 13.0 %collective-permute-start.14 = (f32[4,16]{1,0:T(4,128)}, f32[4,16]{1,0:T(4,128)}, u32[]{:S(2)}, u32[]{:S(2)}) collective-permute-start(f32[4,16]{1,0:T(4,128)} %mul.469), channel_id=1, source_target_pairs={{0,32},{8,40},{16,48},{24,56},{32,64},{40,72},{48,80},{56,88},{64,... | collective-permute-start | bytes 776 | tf_op jit(solution)/shard_map/ppermute | solution.py:19
  117.8 7.9 %collective-permute-start.3 = (f32[4,16]{1,0:T(4,128)}, f32[4,16]{1,0:T(4,128)}, u32[]{:S(2)}, u32[]{:S(2)}) collective-permute-start(f32[4,16]{1,0:T(4,128)} %mul.440), channel_id=1, source_target_pairs={{32,0},{40,8},{48,16},{56,24},{64,32},{72,40},{80,48},{88,56},{96,... | collective-permute-start | bytes 776 | tf_op jit(solution)/shard_map/ppermute | solution.py:19
  120.4 7.9 %collective-permute-start.15 = (f32[4,16]{1,0:T(4,128)}, f32[4,16]{1,0:T(4,128)}, u32[]{:S(2)}, u32[]{:S(2)}) collective-permute-start(f32[4,16]{1,0:T(4,128)} %mul.470), channel_id=1, source_target_pairs={{0,64},{8,72},{16,80},{24,88},{32,96},{40,104},{48,112},{56,120},{... | collective-permute-start | bytes 776 | tf_op jit(solution)/shard_map/ppermute | solution.py:19
  127.0 12.1 %collective-permute-start.4 = (f32[4,16]{1,0:T(4,128)}, f32[4,16]{1,0:T(4,128)}, u32[]{:S(2)}, u32[]{:S(2)}) collective-permute-start(f32[4,16]{1,0:T(4,128)} %mul.441), channel_id=1, source_target_pairs={{64,0},{72,8},{80,16},{88,24},{96,32},{104,40},{112,48},{120,56},{... | collective-permute-start | bytes 776 | tf_op jit(solution)/shard_map/ppermute | solution.py:19
  129.0 111.9 %collective-permute-start.16 = (f32[4,16]{1,0:T(4,128)S(1)}, f32[4,16]{1,0:T(4,128)}, u32[]{:S(2)}, u32[]{:S(2)}) collective-permute-start(f32[4,16]{1,0:T(4,128)S(1)} %mul.471), channel_id=1, source_target_pairs={{0,8},{8,16},{16,24},{24,32},{32,40},{40,48},{48,56},{56,64},{64,7... | collective-permute-start | bytes 776 | tf_op jit(solution)/shard_map/ppermute | solution.py:19
  142.0 28.4 %collective-permute-start.19 = (f32[4,16,32,64]{3,2,1,0:T(8,128)S(1)}, f32[4,16,32,64]{3,2,1,0:T(8,128)S(1)}, u32[]{:S(2)}, u32[]{:S(2)}) collective-permute-start(f32[4,16,32,64]{3,2,1,0:T(8,128)S(1)} %multiply_add_fusion.3), channel_id=1, source_target_pairs={{0,32},{8,40},{16,48},{24,56},{32,64},{40,72},{48,80},{56,88},{64,... | collective-permute-start | bytes 1572872 | tf_op jit(solution)/shard_map/ppermute | solution.py:19
  149.6 28.9 %collective-permute-start.8 = (f32[4,16,32,64]{3,2,1,0:T(8,128)S(1)}, f32[4,16,32,64]{3,2,1,0:T(8,128)S(1)}, u32[]{:S(2)}, u32[]{:S(2)}) collective-permute-start(f32[4,16,32,64]{3,2,1,0:T(8,128)S(1)} %multiply_add_fusion.10), channel_id=1, source_target_pairs={{32,0},{40,8},{48,16},{56,24},{64,32},{72,40},{80,48},{88,56},{96,... | collective-permute-start | bytes 1572872 | tf_op jit(solution)/shard_map/ppermute | solution.py:19
  171.3 29.1 %collective-permute-start.20 = (f32[4,16,32,64]{3,2,1,0:T(8,128)S(1)}, f32[4,16,32,64]{3,2,1,0:T(8,128)S(1)}, u32[]{:S(2)}, u32[]{:S(2)}) collective-permute-start(f32[4,16,32,64]{3,2,1,0:T(8,128)S(1)} %multiply_add_fusion.2), channel_id=1, source_target_pairs={{0,64},{8,72},{16,80},{24,88},{32,96},{40,104},{48,112},{56,120},{... | collective-permute-start | bytes 1572872 | tf_op jit(solution)/shard_map/ppermute | solution.py:19
  179.3 48.0 %collective-permute-start.9 = (f32[4,16,32,64]{3,2,1,0:T(8,128)S(1)}, f32[4,16,32,64]{3,2,1,0:T(8,128)S(1)}, u32[]{:S(2)}, u32[]{:S(2)}) collective-permute-start(f32[4,16,32,64]{3,2,1,0:T(8,128)S(1)} %multiply_add_fusion.9), channel_id=1, source_target_pairs={{64,0},{72,8},{80,16},{88,24},{96,32},{104,40},{112,48},{120,56},{... | collective-permute-start | bytes 1572872 | tf_op jit(solution)/shard_map/ppermute | solution.py:19
  202.2 85.8 %collective-permute-start.21 = (f32[4,16,32,64]{3,2,1,0:T(8,128)}, f32[4,16,32,64]{3,2,1,0:T(8,128)}, u32[]{:S(2)}, u32[]{:S(2)}) collective-permute-start(f32[4,16,32,64]{3,2,1,0:T(8,128)} %multiply_add_fusion.1), channel_id=1, source_target_pairs={{0,136},{8,144},{16,152},{24,160},{32,168},{40,176},{48,184},{56,1... | collective-permute-start | bytes 1572872 | tf_op jit(solution)/shard_map/ppermute | solution.py:19
  212.9 75.1 %collective-permute-start.22 = (f32[4,16,32,64]{3,2,1,0:T(8,128)}, f32[4,16,32,64]{3,2,1,0:T(8,128)}, u32[]{:S(2)}, u32[]{:S(2)}) collective-permute-start(f32[4,16,32,64]{3,2,1,0:T(8,128)} %multiply_add_fusion.1), channel_id=1, source_target_pairs={{0,8},{8,16},{16,24},{24,32},{32,40},{40,48},{48,56},{56,64},{64,7... | collective-permute-start | bytes 1572872 | tf_op jit(solution)/shard_map/ppermute | solution.py:19
  229.3 58.8 %collective-permute-start.10 = (f32[4,16,32,64]{3,2,1,0:T(8,128)}, f32[4,16,32,64]{3,2,1,0:T(8,128)}, u32[]{:S(2)}, u32[]{:S(2)}) collective-permute-start(f32[4,16,32,64]{3,2,1,0:T(8,128)} %multiply_add_fusion.8), channel_id=1, source_target_pairs={{136,0},{144,8},{152,16},{160,24},{168,32},{176,40},{184,48},{192,... | collective-permute-start | bytes 1572872 | tf_op jit(solution)/shard_map/ppermute | solution.py:19
  230.6 57.5 %collective-permute-start.11 = (f32[4,16,32,64]{3,2,1,0:T(8,128)}, f32[4,16,32,64]{3,2,1,0:T(8,128)}, u32[]{:S(2)}, u32[]{:S(2)}) collective-permute-start(f32[4,16,32,64]{3,2,1,0:T(8,128)} %multiply_add_fusion.8), channel_id=1, source_target_pairs={{8,0},{16,8},{24,16},{32,24},{40,32},{48,40},{56,48},{64,56},{72,6... | collective-permute-start | bytes 1572872 | tf_op jit(solution)/shard_map/ppermute | solution.py:19
  240.9 47.2 %collective-permute-start.5 = (f32[4,16]{1,0:T(4,128)}, f32[4,16]{1,0:T(4,128)}, u32[]{:S(2)}, u32[]{:S(2)}) collective-permute-start(f32[4,16]{1,0:T(4,128)} %mul.442), channel_id=1, source_target_pairs={{8,0},{16,8},{24,16},{32,24},{40,32},{48,40},{56,48},{64,56},{72,6... | collective-permute-start | bytes 776 | tf_op jit(solution)/shard_map/ppermute | solution.py:19
  246.9 44.5 %copy-start.2 = (f32[128,2048]{0,1:T(8,128)S(1)}, f32[128,2048]{0,1:T(8,128)}, u32[]{:S(2)}) copy-start(f32[128,2048]{0,1:T(8,128)} %copy-done) | copy-start | bytes 3145732
  246.9 44.5 %copy-start.11 = (f32[4,64,128]{2,1,0:T(8,128)S(1)}, f32[4,64,128]{2,1,0:T(8,128)}, u32[]{:S(2)}) copy-start(f32[4,64,128]{2,1,0:T(8,128)} %fusion.55) | copy-start | bytes 393220
  305.5 110.1 %copy-start.3 = (f32[128,2560]{0,1:T(8,128)S(1)}, f32[128,2560]{0,1:T(8,128)}, u32[]{:S(2)}) copy-start(f32[128,2560]{0,1:T(8,128)} %get-tuple-element.63) | copy-start | bytes 3932164
  416.0 6.8 %collective-permute-start.23 = (f32[3,2560]{1,0:T(4,128)S(1)}, f32[3,2560]{1,0:T(4,128)S(1)}, u32[]{:S(2)}, u32[]{:S(2)}) collective-permute-start(f32[3,2560]{1,0:T(4,128)S(1)} %copy.142), channel_id=1, source_target_pairs={{8,0},{16,8},{24,16},{32,24},{40,32},{48,40},{56,48},{64,56},{72,6... | collective-permute-start | bytes 92168 | tf_op jit(solution)/shard_map/ppermute | solution.py:19
  (31 other events, 169.2 us)
